TPU v7x, 256 devices: a whole 4x4x8 slice. The times are simulated.
256 devices in a mesh: req: 32 (over z, y), mdl: 8 (over x, core).
Axes of the slice: x: 4, y: 4, z: 8, core: 2. Of those that a mesh axis runs over, the one named last changes fastest.
Arguments:
- stream: bfloat16 [24576, 1792], P('req'), may hold values from -6 to 6
- attention_projection_weight: bfloat16 [3, 1792, 1792], P(None, 'mdl'), may hold values from -0.125 to 0.125
- head_output_weight: bfloat16 [1792, 1792], P('mdl'), may hold values from -0.125 to 0.125
- adapter_down_maps: bfloat16 [64, 1792, 16], P('mdl'), may hold values from -0.125 to 0.125
- adapter_up_maps: bfloat16 [2, 1792, 1024], P(None, 'mdl'), may hold values from -1.5 to 1.5
- tenant_adapter_scale: float32 [4], replicated, may hold values from 0.5 to 2
- feedforward_norm_gain: bfloat16 [1792], replicated, may hold values from 0.099609375 to 1.8984375
- feedforward_weight: bfloat16 [3, 1792, 4864], P(None, 'req', 'mdl'), may hold values from -0.125 to 0.125
- prefix_cache_store: bfloat16 [1024, 2, 1792, 128], P('req', None, 'mdl'), may hold values from -140 to 140
- token_adapter_index: int32 [24576], P('req'), may hold values from 0 to 63
- request_token_lengths: int32 [32, 24], P('req'), may hold values from 1 to 192, 768 in all within a row
- request_tenant_index: int32 [768], P('req'), may hold values from 0 to 3
- last_page_holder: int32 [768, 1], replicated, may hold values from 0 to 31; in each aligned block of 24 rows (0 to 23, 24 to 47, ...) at most 2 rows name the same one
- holder_page_slot: int32 [768], replicated, may hold values from 0 to 31
- page_filled_rows: int32 [768], replicated, may hold values from 64 to 128
Outputs:
- layer_out: bfloat16 [24576, 1792], P(('req', 'mdl'))
Inputs may be any that keep to these rules, and one draw needn't show every extreme that they name: `last_page_holder`: within the rows of one index of req (aligned blocks of 24 rows) no holder is named more than 2 times, and one holder exactly 2 times in some blocks. `request_token_lengths`: each row sums to 768; its longest request has exactly 192 tokens.
All inputs are finite; a program needn't handle non-finite values.
Results may differ from a plain program's by a relative error of at most 0.025.
Values may be sent and summed in bfloat16 or wider, within the bound.
A program may use at most 128 MiB of HBM per device.

v0:
```python
import math
import jax
import jax.numpy as jnp
from jax import lax
from jax.sharding import PartitionSpec as P

HEAD_SIZE = 112
WINDOW = 64


def per_device(
    stream,
    attention_projection_weight,
    head_output_weight,
    adapter_down_maps,
    adapter_up_maps,
    tenant_adapter_scale,
    feedforward_norm_gain,
    feedforward_weight,
    prefix_cache_store,
    token_adapter_index,
    request_token_lengths,
    request_tenant_index,
    last_page_holder,
    holder_page_slot,
    page_filled_rows,
):
    tok_count, model_width = stream.shape
    head_column_set = attention_projection_weight.shape[1]
    head_local = head_column_set // HEAD_SIZE
    req_per_dev = request_token_lengths.shape[1]
    rank_total_width = adapter_down_maps.shape[2]
    adapter_number = adapter_up_maps.shape[2] // rank_total_width
    req_devices = lax.axis_size("req")
    req_index = lax.axis_index("req")
    mdl_index = lax.axis_index("mdl")
    row_share = tok_count // lax.axis_size("mdl")
    cap_slots = max(2, (req_per_dev + req_devices - 1) // req_devices + 1)
    projected_rows = jnp.einsum(
        "td,kcd->ktc", stream, attention_projection_weight, preferred_element_type=jnp.float32
    )
    all_onehot = (
        token_adapter_index[:, None] == jnp.arange(adapter_number, dtype=jnp.int32)[None, :]
    )
    holder_count = adapter_down_maps.shape[0]
    holder_rank_rows = jnp.einsum(
        "qf,kfn->qkn", stream, adapter_down_maps, preferred_element_type=jnp.float32
    )
    held_onehot = (
        token_adapter_index[:, None]
        == (mdl_index * holder_count + jnp.arange(holder_count, dtype=jnp.int32))[None, :]
    )
    rank_part = jnp.sum(holder_rank_rows * held_onehot.astype(jnp.float32)[:, :, None], axis=1)
    rank_feat = lax.psum(rank_part.astype(jnp.bfloat16), "mdl")
    broadcast_result = (
        all_onehot.astype(jnp.bfloat16)[:, :, None] * rank_feat[:, None, :]
    ).reshape(tok_count, adapter_number * rank_total_width)
    adapter_column_set = jnp.einsum(
        "iu,pdu->ipd", broadcast_result, adapter_up_maps, preferred_element_type=jnp.float32
    )
    positions = jnp.arange(tok_count, dtype=jnp.int32)
    lengths_row = request_token_lengths[0]
    starts = jnp.cumsum(lengths_row) - lengths_row
    member = (positions[:, None] >= starts[None, :]) & (
        positions[:, None] < (starts + lengths_row)[None, :]
    )
    member_int = member.astype(jnp.int32)
    request_of = jnp.sum(member_int * jnp.arange(req_per_dev, dtype=jnp.int32)[None, :], axis=1)
    relative = positions - jnp.sum(member_int * starts[None, :], axis=1)
    tenant_hot = (
        request_tenant_index[:, None]
        == jnp.arange(tenant_adapter_scale.shape[0], dtype=jnp.int32)[None, :]
    ).astype(jnp.float32)
    request_scale = jnp.sum(tenant_hot * tenant_adapter_scale[None, :], axis=1)
    per_token_scale = jnp.sum(member.astype(jnp.float32) * request_scale[None, :], axis=1)[:, None]
    query_rows = (projected_rows[0] + per_token_scale * adapter_column_set[:, 0]).astype(
        jnp.bfloat16
    )
    key_rows = projected_rows[1].astype(jnp.bfloat16)
    value_row_block = (projected_rows[2] + per_token_scale * adapter_column_set[:, 1]).astype(
        jnp.bfloat16
    )
    owner_column = last_page_holder[:, 0]
    owner_table = owner_column.reshape(req_devices, req_per_dev)
    slot_table = holder_page_slot.reshape(req_devices, req_per_dev)
    owned = (owner_table == req_index).astype(jnp.int32)
    owned_rank = jnp.cumsum(owned, axis=1) - 1
    picked = owned[:, None, :] * (
        owned_rank[:, None, :] == jnp.arange(cap_slots, dtype=jnp.int32)[None, :, None]
    ).astype(jnp.int32)
    send_slot = jnp.sum(picked * slot_table[:, None, :], axis=2)
    fill_table = page_filled_rows.reshape(req_devices, req_per_dev)
    send_fill = jnp.sum(picked * fill_table[:, None, :], axis=2)
    my_owner = lax.dynamic_slice_in_dim(owner_column, req_index * req_per_dev, req_per_dev, 0)
    order_ids = jnp.arange(req_per_dev, dtype=jnp.int32)
    earlier = (my_owner[:, None] == my_owner[None, :]) & (order_ids[:, None] > order_ids[None, :])
    flat_pick = my_owner * cap_slots + jnp.sum(earlier.astype(jnp.int32), axis=1)
    page_inner = prefix_cache_store.shape[1:3]

    def cut_window(slot, fill):
        return lax.dynamic_slice(
            prefix_cache_store, (slot, 0, 0, fill - WINDOW), (1,) + page_inner + (WINDOW,)
        )[0]

    source_pages = jax.vmap(cut_window)(send_slot.reshape(-1), send_fill.reshape(-1))
    source_pages = source_pages.reshape((req_devices, cap_slots) + page_inner + (WINDOW,))
    arrived = lax.all_to_all(source_pages, "req", split_axis=0, concat_axis=0, tiled=True)
    full_mlp = lax.all_gather(feedforward_weight, "req", axis=1, tiled=True)
    full_mlp, arrived = lax.optimization_barrier((full_mlp, arrived))
    chosen = jnp.take(
        arrived.reshape((req_devices * cap_slots,) + page_inner + (WINDOW,)),
        flat_pick,
        axis=0,
        mode="clip",
    )
    prefix = jnp.transpose(chosen, (0, 3, 1, 2))
    key_all = jnp.concatenate(
        [key_rows, prefix[:, :, 0].reshape(req_per_dev * WINDOW, head_column_set)], axis=0
    )
    value_all = jnp.concatenate(
        [value_row_block, prefix[:, :, 1].reshape(req_per_dev * WINDOW, head_column_set)], axis=0
    )
    distance = positions[:, None] - positions[None, :]
    local_ok = (request_of[:, None] == request_of[None, :]) & (distance >= 0) & (distance <= WINDOW)
    key_request = jnp.repeat(jnp.arange(req_per_dev, dtype=jnp.int32), WINDOW)
    key_offset = jnp.tile(jnp.arange(WINDOW, dtype=jnp.int32), req_per_dev)
    prefix_ok = (request_of[:, None] == key_request[None, :]) & (
        key_offset[None, :] >= relative[:, None]
    )
    allowed = jnp.concatenate([local_ok, prefix_ok], axis=1)
    query_heads = query_rows.reshape(tok_count, head_local, HEAD_SIZE)
    key_heads = key_all.reshape(-1, head_local, HEAD_SIZE)
    value_heads = value_all.reshape(-1, head_local, HEAD_SIZE)
    scores = jnp.einsum(
        "thd,shd->hts", query_heads, key_heads, preferred_element_type=jnp.float32
    ) * (1.0 / math.sqrt(HEAD_SIZE))
    masked = jnp.where(allowed[None], scores, -1e30)
    row_max = jnp.max(masked, axis=-1, keepdims=True)
    exp_scores = jnp.exp(masked - row_max)
    weights = (exp_scores / jnp.sum(exp_scores, axis=-1, keepdims=True)).astype(jnp.bfloat16)
    mixed = (
        jnp.einsum("hts,shd->thd", weights, value_heads, preferred_element_type=jnp.float32)
        .astype(jnp.bfloat16)
        .reshape(tok_count, head_column_set)
    )
    attn_part = (
        jnp.dot(mixed, head_output_weight, preferred_element_type=jnp.float32)
        .astype(jnp.bfloat16)
        .astype(jnp.float32)
    )
    gain_wide = feedforward_norm_gain.astype(jnp.float32)[None, :]
    attn_full = lax.psum(attn_part.astype(jnp.bfloat16), "mdl").astype(jnp.float32)
    resid_full = (stream.astype(jnp.float32) + attn_full).astype(jnp.bfloat16)
    resid_wide = resid_full.astype(jnp.float32)
    mean_sq = jnp.mean(resid_wide * resid_wide, axis=1, keepdims=True)
    normed = (resid_wide * lax.rsqrt(mean_sq + 1e-06) * gain_wide).astype(jnp.bfloat16)
    resid_mine = lax.dynamic_slice_in_dim(resid_full, mdl_index * row_share, row_share, 0)
    gate_part = jnp.dot(normed, full_mlp[0], preferred_element_type=jnp.float32)
    up_part = jnp.dot(normed, full_mlp[1], preferred_element_type=jnp.float32)
    hidden = (jax.nn.silu(gate_part) * up_part).astype(jnp.bfloat16)
    mlp_part = (
        jnp.einsum("tf,df->td", hidden, full_mlp[2], preferred_element_type=jnp.float32)
        .astype(jnp.bfloat16)
        .astype(jnp.float32)
    )
    mlp_mine = lax.psum_scatter(
        mlp_part.astype(jnp.bfloat16), "mdl", scatter_dimension=0, tiled=True
    ).astype(jnp.float32)
    return (resid_mine.astype(jnp.float32) + mlp_mine).astype(jnp.bfloat16)


def solution(mesh):
    return jax.shard_map(
        per_device,
        mesh=mesh,
        in_specs=(
            P("req", None),
            P(None, "mdl", None),
            P("mdl", None),
            P("mdl", None, None),
            P(None, "mdl", None),
            P(),
            P(),
            P(None, "req", "mdl"),
            P("req", None, "mdl", None),
            P("req"),
            P("req", None),
            P("req"),
            P(),
            P(),
            P(),
        ),
        out_specs=P(("req", "mdl"), None),
        check_vma=False,
    )
```

profile of v0, /device:TPU:8, one launch (start us, length us, event | category | flops | bytes accessed | tf_op | source)
XLA Modules:
  0.0 343.1 jit_solution(13836156589425205847)
XLA Ops:
  10.7 11.2 %copy.33 = bf16[32,2,224,128]{2,1,0,3:T(2,128)(2,1)} copy(bf16[32,2,224,128]{3,2,1,0:T(8,128)(2,1)} %param.23) | data formatting | bytes 7340032 | tf_op args[8]
  21.9 14.3 %gather_fusion = bf16[64,2,224,64]{2,1,3,0:T(2,128)(2,1)} fusion(bf16[32,2,224,128]{2,1,0,3:T(2,128)(2,1)} %copy.33, s32[64]{0:T(128)S(1)} %fusion.53), kind=kCustom, calls=%fused_computation | custom fusion | bytes 7341056 | tf_op jit(solution)/shard_map/vmap()/gather | solution.py:101
  36.2 12.9 %all-to-all-start = ((bf16[32,2,2,224,64]{3,2,4,1,0:T(2,128)(2,1)}), bf16[32,2,2,224,64]{3,2,4,1,0:T(2,128)(2,1)}, u32[]{:S(2)}, u32[]{:S(2)}) async-start(bf16[32,2,2,224,64]{3,2,4,1,0:T(2,128)(2,1)} %bitcast.72), calls=%async_computation | async-start | bytes 8388608 | tf_op jit(solution)/shard_map/all_to_all | solution.py:107
  49.6 3.9 %fusion.23 = f32[3,768,224]{1,2,0:T(8,128)S(1)} fusion(bf16[3,224,1792]{2,1,0:T(8,128)(2,1)S(1)} %copy-done, bf16[768,1792]{1,0:T(8,128)(2,1)} %param.15), kind=kOutput, calls=%fused_computation.37 | convolution fusion | flops 1849688064 | bytes 7225344 | tf_op jit(solution)/shard_map/td,kcd->ktc/dot_general | solution.py:39
  53.6 1.4 copy-done.3
  55.1 2.8 fusion.67
  58.0 26.8 %psum.14 = bf16[768,16]{0,1:T(8,128)(2,1)S(1)} all-reduce(bf16[768,16]{0,1:T(8,128)(2,1)S(1)} %multiply_reduce_fusion), channel_id=1, replica_groups=mesh['req'=32,'mdl'=8] {'mdl'}, use_global_device_ids=true, to_apply=%region_4.5 | all-reduce | flops 12288 | bytes 49152 | tf_op jit(solution)/shard_map/psum | solution.py:54
  86.9 1.4 fusion.63
  89.6 1.1 add_convert_fusion.3
  90.7 1.3 compare_and_fusion
  91.9 1.4 pad_add_fusion
  93.3 81.0 %all-to-all-done = bf16[32,2,2,224,64]{3,2,4,1,0:T(2,128)(2,1)} async-done(((bf16[32,2,2,224,64]{3,2,4,1,0:T(2,128)(2,1)}), bf16[32,2,2,224,64]{3,2,4,1,0:T(2,128)(2,1)}, u32[]{:S(2)}, u32[]{:S(2)}) %all-to-all-start) | async-done | bytes 3670048 | tf_op jit(solution)/shard_map/all_to_all | solution.py:107
  174.3 5.1 %copy.34 = bf16[32,2,2,224,64]{3,4,2,1,0:T(8,128)(2,1)} copy(bf16[32,2,2,224,64]{3,2,4,1,0:T(2,128)(2,1)} %all-to-all-done) | data formatting | bytes 7340032 | tf_op jit(solution)/shard_map/optimization_barrier | solution.py:109
  179.4 2.8 gather_fusion.1
  184.5 9.5 %fusion.66 = (f32[2,768]{1,0:T(2,128)S(1)}, f32[2,768,2304]{2,1,0:T(8,128)}) fusion(pred[768,2304]{1,0:T(8,128)(4,1)} %pad_add_fusion, bf16[768,2,112]{0,2,1:T(8,128)(2,1)S(1)} %copy-done.7, bf16[1536,2,112]{0,2,1:T(8,128)(2,1)S(1)} %copy.36, bf16[768,2,112]{0,2,1:T(8,128)(2,1)S(1)} %bitcast.82), kind=kOutput, calls=%fused_computation.102 | convolution fusion | flops 808945920 | bytes 17307648 | tf_op jit(solution)/shard_map/sub | solution.py:139
  194.1 7.6 %fusion.32 = bf16[2,112,768]{2,1,0:T(8,128)(2,1)S(1)} fusion(f32[2,768,2304]{2,1,0:T(8,128)} %get-tuple-element.26, f32[2,768]{1,0:T(2,128)S(1)} %get-tuple-element.25, bf16[1536,2,112]{0,2,1:T(8,128)(2,1)S(1)} %copy.35, bf16[768,2,112]{0,2,1:T(8,128)(2,1)S(1)} %copy-done.6), kind=kOutput, calls=%fused_computation.39 | convolution fusion | flops 802037760 | bytes 15538176 | tf_op jit(solution)/shard_map/hts,shd->thd/dot_general | solution.py:142
  201.7 2.5 convolution_convert_fusion
  204.5 72.0 %all-reduce.2.cloned.1.call-done = bf16[768,1792]{1,0:T(8,128)(2,1)} async-done(((bf16[768,1792]{1,0:T(8,128)(2,1)}), bf16[768,1792]{1,0:T(8,128)(2,1)}) %all-reduce.2.cloned.1.call-update) | async-done | bytes 2752528 | tf_op jit(solution)/shard_map/psum | solution.py:152
  276.4 3.7 %fusion.6 = (f32[768]{0:T(1024)S(1)}, bf16[768,1792]{1,0:T(8,128)(2,1)S(1)}) fusion(bf16[768,1792]{1,0:T(8,128)(2,1)} %all-reduce.2.cloned.1.call-done, bf16[768,1792]{1,0:T(8,128)(2,1)} %param.15), kind=kLoop, calls=%fused_computation.14 | loop fusion | flops 9633024 | bytes 8260608 | tf_op jit(solution)/shard_map/reduce_sum | solution.py:155
  280.1 1.5 copy-done.2
  281.7 5.1 %fusion.18 = f32[768,608]{0,1:T(8,128)} fusion(bf16[3,1792,608]{2,1,0:T(8,128)(2,1)} %all-gather.2.cloned.1.call-done, bf16[768,1792]{1,0:T(8,128)(2,1)S(1)} %get-tuple-element.14, f32[1792]{0:T(1024)S(1)} %convert_element_type.118, f32[768]{0:T(1024)S(1)} %add_rsqrt_fusion), kind=kOutput, calls=%fused_computation.31 | convolution fusion | flops 1679032320 | bytes 6924288 | tf_op jit(solution)/shard_map/dot_general | solution.py:158
  286.7 10.6 %convolution_convert_fusion.1 = bf16[768,1792]{1,0:T(8,128)(2,1)} fusion(bf16[3,1792,608]{2,1,0:T(8,128)(2,1)} %all-gather.2.cloned.1.call-done, f32[768,608]{0,1:T(8,128)} %fusion.18, bf16[768,1792]{1,0:T(8,128)(2,1)} %copy-done.2, f32[1792]{0:T(1024)S(1)} %convert_element_type.118, f32[768]{0:T(1024)S(1)} %add_rsqrt_fusion), kind=kOutput, calls=%fused_computation.20 | convolution fusion | flops 3356737536 | bytes 11970560 | tf_op jit(solution)/shard_map/tf,df->td/dot_general | solution.py:162
  297.4 37.3 %reduce-scatter.2.cloned.1.call-done = bf16[96,1792]{1,0:T(8,128)(2,1)} async-done(((bf16[768,1792]{1,0:T(8,128)(2,1)}), bf16[96,1792]{1,0:T(8,128)(2,1)}) %reduce-scatter.2.cloned.1.call-update) | async-done | bytes 344080 | tf_op jit(solution)/shard_map/reduce_scatter | solution.py:166
  334.7 1.9 add_convert_fusion.1
  (84 shorter events, 10.7 us)
Async XLA Ops:
  6.5 43.1 %copy-start = (bf16[3,224,1792]{2,1,0:T(8,128)(2,1)S(1)}, bf16[3,224,1792]{2,1,0:T(8,128)(2,1)}, u32[]{:S(2)}) copy-start(bf16[3,224,1792]{2,1,0:T(8,128)(2,1)} %param.16) | copy-start | bytes 7225348
  6.5 167.8 %all-gather.2.cloned.1.call-start = ((), (), s32[]{:S(2)}) async-start(), calls=%async_computation.2 | async-start | bytes 7096320 | tf_op jit(solution)/shard_map/all_gather | solution.py:108
  36.2 13.0 %copy-start.10 = (s32[1,24]{1,0:T(1,128)S(1)}, s32[1,24]{1,0:T(1,128)}, u32[]{:S(2)}) copy-start(s32[1,24]{1,0:T(1,128)} %param.25) | copy-start | bytes 292
  36.2 138.1 %all-to-all-start = ((bf16[32,2,2,224,64]{3,2,4,1,0:T(2,128)(2,1)}), bf16[32,2,2,224,64]{3,2,4,1,0:T(2,128)(2,1)}, u32[]{:S(2)}, u32[]{:S(2)}) async-start(bf16[32,2,2,224,64]{3,2,4,1,0:T(2,128)(2,1)} %bitcast.72), calls=%async_computation | async-start | bytes 8388608 | tf_op jit(solution)/shard_map/all_to_all | solution.py:107
  49.2 227.3 %all-reduce.2.cloned.1.call-start = ((), (), s32[]{:S(2)}) async-start(), calls=%async_computation.3 | async-start | bytes 5505024 | tf_op jit(solution)/shard_map/psum | solution.py:152
  49.6 5.4 %copy-start.8 = (s32[768]{0:T(1024)S(1)}, s32[768]{0:T(1024)}, u32[]{:S(2)}) copy-start(s32[768]{0:T(1024)} %param.24) | copy-start | bytes 9220
  49.6 5.4 %copy-start.5 = (bf16[8,1792,16]{1,2,0:T(8,128)(2,1)S(1)}, bf16[8,1792,16]{1,2,0:T(8,128)(2,1)}, u32[]{:S(2)}) copy-start(bf16[8,1792,16]{1,2,0:T(8,128)(2,1)} %param.18) | copy-start | bytes 1376260
  53.6 1.4 copy-start.3
  55.0 31.5 %copy-start.12 = (f32[4]{0:T(128)S(1)}, f32[4]{0:T(128)}, u32[]{:S(2)}) copy-start(f32[4]{0:T(128)} %param.20) | copy-start | bytes 52
  55.0 31.4 %copy-start.13 = (s32[24]{0:T(128)S(1)}, s32[24]{0:T(128)}, u32[]{:S(2)}) copy-start(s32[24]{0:T(128)} %param.26) | copy-start | bytes 292
  57.9 30.4 %copy-start.11 = (bf16[2,224,1024]{2,1,0:T(8,128)(2,1)S(1)}, bf16[2,224,1024]{2,1,0:T(8,128)(2,1)}, u32[]{:S(2)}) copy-start(bf16[2,224,1024]{2,1,0:T(8,128)(2,1)} %param.19) | copy-start | bytes 2752516
  182.9 1.6 copy-start.7
  184.5 9.6 %copy-start.6 = (bf16[768,2,112]{0,2,1:T(8,128)(2,1)S(1)}, bf16[768,2,112]{0,2,1:T(8,128)(2,1)}, u32[]{:S(2)}) copy-start(bf16[768,2,112]{0,2,1:T(8,128)(2,1)} %get-tuple-element.21) | copy-start | bytes 1032196
  194.1 7.6 %copy-start.4 = (bf16[224,1792]{1,0:T(8,128)(2,1)S(1)}, bf16[224,1792]{1,0:T(8,128)(2,1)}, u32[]{:S(2)}) copy-start(bf16[224,1792]{1,0:T(8,128)(2,1)} %param.17) | copy-start | bytes 2408452
  201.6 2.8 copy-start.9
  204.2 130.5 %reduce-scatter.2.cloned.1.call-start = ((), (), s32[]{:S(2)}) async-start(), calls=%async_computation.4 | async-start | bytes 3096576 | tf_op jit(solution)/shard_map/reduce_scatter | solution.py:166
  280.1 1.6 copy-start.2
  286.7 49.9 %copy-start.1 = (bf16[3,224,1792]{2,1,0:T(8,128)(2,1)S(1)}, bf16[3,224,1792]{2,1,0:T(8,128)(2,1)}, u32[]{:S(2)}) copy-start(bf16[3,224,1792]{2,1,0:T(8,128)(2,1)} %param.16) | copy-start | bytes 7225348
Sparse Core Ops, SparseCore 0:
  10.0 159.9 all-gather.1
  204.3 72.0 all-reduce.1
  297.5 37.1 reduce-scatter.1
where the time goes:
time: 344 us; the launch traced here: 343 us
  waiting for transfers between devices  191 us (56%)
  local copies, waits for them, and re-layouts  43.6 us (13%)
  matrix products  42.9 us (12%)
  blocking collectives  26.8 us (8%)
  between operations  13.5 us (4%)
  starting transfers between devices  13.2 us (4%)
  other arithmetic  12.1 us (4%)
    all_to_all x1, waiting for transfers between devices, per_device(): lax.all_to_all(source_pages, 'req', split_axis=0, concat_axis=0, tiled=True)  81 us
    psum x1, waiting for transfers between devices, per_device(): lax.psum(attn_part.astype(jnp.bfloat16), 'mdl').astype(jnp.float32)  72 us
    reduce_scatter x1, waiting for transfers between devices, per_device(): lax.psum_scatter(mlp_part.astype(jnp.bfloat16), 'mdl', scatter_dimension=...  37.3 us
    psum x1, blocking collectives, per_device(): rank_feat = lax.psum(rank_part.astype(jnp.bfloat16), 'mdl')  26.8 us
    gather x1, local copies, waits for them, and re-layouts, cut_window(): lax.dynamic_slice(prefix_cache_store, (slot, 0, 0, fill - WINDOW), (1,) +...  14.3 us
    unnamed x29, local copies, waits for them, and re-layouts  14.2 us
    all_to_all x1, starting transfers between devices, per_device(): lax.all_to_all(source_pages, 'req', split_axis=0, concat_axis=0, tiled=True)  12.9 us
    dot_general x1, matrix products, per_device(): jnp.einsum('tf,df->td', hidden, full_mlp[2], preferred_element_type=jnp.f...  10.6 us
  transfers between devices with their start and end apart: 4, of which 3 were waited for; matrix products, arithmetic and copies ran while one was open for 13% of the time, Pallas kernels for 0%

commit v1 on v0

--- a/solution.py
+++ b/solution.py
@@ -51,7 +51,7 @@
         == (mdl_index * holder_count + jnp.arange(holder_count, dtype=jnp.int32))[None, :]
     )
     rank_part = jnp.sum(holder_rank_rows * held_onehot.astype(jnp.float32)[:, :, None], axis=1)
-    rank_feat = lax.psum(rank_part.astype(jnp.bfloat16), "mdl")
+    rank_feat = jnp.sum(lax.all_gather(rank_part.astype(jnp.bfloat16), "mdl"), axis=0)
     broadcast_result = (
         all_onehot.astype(jnp.bfloat16)[:, :, None] * rank_feat[:, None, :]
     ).reshape(tok_count, adapter_number * rank_total_width)

time: 344 us -> 344 us (level)
  waiting for transfers between devices: 191 us -> 205 us
  blocking collectives: 26.8 us -> 13.4 us
    psum x1 -> x0, blocking collectives: 26.8 us -> none  [per_device(): rank_feat = lax.psum(rank_part.astype(jnp.bfloat16), 'mdl')]
    all_to_all x1, waiting for transfers between devices: 81 us -> 94.7 us  [per_device(): lax.all_to_all(source_pages, 'req', split_axis=0, concat_axis=0, tiled=True)]
    all_gather x0 -> x1, blocking collectives: none -> 13.4 us  [per_device(): lax.all_gather(rank_part.astype(jnp.bfloat16), 'mdl')]
    unnamed x29 -> x30, local copies, waits for them, and re-layouts: 14.2 us -> 14.2 us
where the time goes in v1:
time: 344 us; the launch traced here: 343 us
  waiting for transfers between devices  205 us (60%)
  local copies, waits for them, and re-layouts  43.6 us (13%)
  matrix products  42.4 us (12%)
  between operations  13.5 us (4%)
  blocking collectives  13.4 us (4%)
  starting transfers between devices  13.2 us (4%)
  other arithmetic  12.3 us (4%)
    all_to_all x1, waiting for transfers between devices, per_device(): lax.all_to_all(source_pages, 'req', split_axis=0, concat_axis=0, tiled=True)  94.7 us
    psum x1, waiting for transfers between devices, per_device(): lax.psum(attn_part.astype(jnp.bfloat16), 'mdl').astype(jnp.float32)  72.2 us
    reduce_scatter x1, waiting for transfers between devices, per_device(): lax.psum_scatter(mlp_part.astype(jnp.bfloat16), 'mdl', scatter_dimension=...  37.4 us
    gather x1, local copies, waits for them, and re-layouts, cut_window(): lax.dynamic_slice(prefix_cache_store, (slot, 0, 0, fill - WINDOW), (1,) +...  14.3 us
    unnamed x30, local copies, waits for them, and re-layouts  14.2 us
    all_gather x1, blocking collectives, per_device(): lax.all_gather(rank_part.astype(jnp.bfloat16), 'mdl')  13.4 us
    all_to_all x1, starting transfers between devices, per_device(): lax.all_to_all(source_pages, 'req', split_axis=0, concat_axis=0, tiled=True)  12.9 us
    dot_general x1, matrix products, per_device(): jnp.einsum('tf,df->td', hidden, full_mlp[2], preferred_element_type=jnp.f...  10.6 us
  transfers between devices with their start and end apart: 4, of which 3 were waited for; matrix products, arithmetic and copies ran while one was open for 13% of the time, Pallas kernels for 0%

profile of v1, /device:TPU:8, one launch (start us, length us, event | category | flops | bytes accessed | tf_op | source)
XLA Modules:
  0.0 343.4 jit_solution(14834773080529675949)
XLA Ops:
  10.7 11.2 %copy.39 = bf16[32,2,224,128]{2,1,0,3:T(2,128)(2,1)} copy(bf16[32,2,224,128]{3,2,1,0:T(8,128)(2,1)} %param.23) | data formatting | bytes 7340032 | tf_op args[8]
  21.9 14.3 %gather_fusion = bf16[64,2,224,64]{2,1,3,0:T(2,128)(2,1)} fusion(bf16[32,2,224,128]{2,1,0,3:T(2,128)(2,1)} %copy.39, s32[64]{0:T(128)S(1)} %fusion.53), kind=kCustom, calls=%fused_computation | custom fusion | bytes 7341056 | tf_op jit(solution)/shard_map/vmap()/gather | solution.py:101
  36.3 12.9 %all-to-all-start = ((bf16[32,2,2,224,64]{3,2,4,1,0:T(2,128)(2,1)}), bf16[32,2,2,224,64]{3,2,4,1,0:T(2,128)(2,1)}, u32[]{:S(2)}, u32[]{:S(2)}) async-start(bf16[32,2,2,224,64]{3,2,4,1,0:T(2,128)(2,1)} %bitcast.77), calls=%async_computation | async-start | bytes 8388608 | tf_op jit(solution)/shard_map/all_to_all | solution.py:107
  49.7 3.0 fusion.67
  52.7 13.4 %all-gather = bf16[6144,16]{0,1:T(8,128)(2,1)S(1)} all-gather(bf16[768,16]{0,1:T(8,128)(2,1)S(1)} %multiply_reduce_fusion), channel_id=2, replica_groups=mesh['req'=32,'mdl'=8] {'mdl'}, dimensions={0}, use_global_device_ids=true | all-gather | bytes 221184 | tf_op jit(solution)/shard_map/all_gather | solution.py:54
  66.2 2.1 fusion.23
  68.2 1.4 copy-done.4
  72.0 1.4 fusion.63
  73.4 2.1 fusion.68
  77.0 1.3 compare_and_fusion
  78.2 1.4 pad_add_fusion
  79.6 94.7 %all-to-all-done = bf16[32,2,2,224,64]{3,2,4,1,0:T(2,128)(2,1)} async-done(((bf16[32,2,2,224,64]{3,2,4,1,0:T(2,128)(2,1)}), bf16[32,2,2,224,64]{3,2,4,1,0:T(2,128)(2,1)}, u32[]{:S(2)}, u32[]{:S(2)}) %all-to-all-start) | async-done | bytes 3670048 | tf_op jit(solution)/shard_map/all_to_all | solution.py:107
  174.4 5.1 %copy.40 = bf16[32,2,2,224,64]{3,4,2,1,0:T(8,128)(2,1)} copy(bf16[32,2,2,224,64]{3,2,4,1,0:T(2,128)(2,1)} %all-to-all-done) | data formatting | bytes 7340032 | tf_op jit(solution)/shard_map/optimization_barrier | solution.py:109
  179.5 2.8 gather_fusion.1
  184.5 9.6 %fusion.66 = (f32[2,768]{1,0:T(2,128)S(1)}, f32[2,768,2304]{2,1,0:T(8,128)}) fusion(pred[768,2304]{1,0:T(8,128)(4,1)} %pad_add_fusion, bf16[768,2,112]{0,2,1:T(8,128)(2,1)S(1)} %copy-done.8, bf16[1536,2,112]{0,2,1:T(8,128)(2,1)S(1)} %copy.42, bf16[768,2,112]{0,2,1:T(8,128)(2,1)S(1)} %bitcast.88), kind=kOutput, calls=%fused_computation.103 | convolution fusion | flops 808945920 | bytes 17307648 | tf_op jit(solution)/shard_map/sub | solution.py:139
  194.1 7.6 %fusion.32 = bf16[2,112,768]{2,1,0:T(8,128)(2,1)S(1)} fusion(f32[2,768,2304]{2,1,0:T(8,128)} %get-tuple-element.26, f32[2,768]{1,0:T(2,128)S(1)} %get-tuple-element.25, bf16[1536,2,112]{0,2,1:T(8,128)(2,1)S(1)} %copy.41, bf16[768,2,112]{0,2,1:T(8,128)(2,1)S(1)} %copy-done.7), kind=kOutput, calls=%fused_computation.39 | convolution fusion | flops 802037760 | bytes 15538176 | tf_op jit(solution)/shard_map/hts,shd->thd/dot_general | solution.py:142
  201.7 2.5 convolution_convert_fusion
  204.5 72.2 %all-reduce.2.cloned.1.call-done = bf16[768,1792]{1,0:T(8,128)(2,1)} async-done(((bf16[768,1792]{1,0:T(8,128)(2,1)}), bf16[768,1792]{1,0:T(8,128)(2,1)}) %all-reduce.2.cloned.1.call-update) | async-done | bytes 2752528 | tf_op jit(solution)/shard_map/psum | solution.py:152
  276.7 3.7 %fusion.6 = (f32[768]{0:T(1024)S(1)}, bf16[768,1792]{1,0:T(8,128)(2,1)S(1)}) fusion(bf16[768,1792]{1,0:T(8,128)(2,1)} %all-reduce.2.cloned.1.call-done, bf16[768,1792]{1,0:T(8,128)(2,1)} %param.15), kind=kLoop, calls=%fused_computation.14 | loop fusion | flops 9633024 | bytes 8260608 | tf_op jit(solution)/shard_map/reduce_sum | solution.py:155
  280.4 1.5 copy-done.3
  281.9 5.1 %fusion.18 = f32[768,608]{0,1:T(8,128)} fusion(bf16[3,1792,608]{2,1,0:T(8,128)(2,1)} %all-gather.3.cloned.1.call-done, bf16[768,1792]{1,0:T(8,128)(2,1)S(1)} %get-tuple-element.14, f32[1792]{0:T(1024)S(1)} %convert_element_type.131, f32[768]{0:T(1024)S(1)} %add_rsqrt_fusion), kind=kOutput, calls=%fused_computation.31 | convolution fusion | flops 1679032320 | bytes 6924288 | tf_op jit(solution)/shard_map/dot_general | solution.py:158
  287.0 10.6 %convolution_convert_fusion.1 = bf16[768,1792]{1,0:T(8,128)(2,1)} fusion(bf16[3,1792,608]{2,1,0:T(8,128)(2,1)} %all-gather.3.cloned.1.call-done, f32[768,608]{0,1:T(8,128)} %fusion.18, bf16[768,1792]{1,0:T(8,128)(2,1)} %copy-done.3, f32[1792]{0:T(1024)S(1)} %convert_element_type.131, f32[768]{0:T(1024)S(1)} %add_rsqrt_fusion), kind=kOutput, calls=%fused_computation.20 | convolution fusion | flops 3356737536 | bytes 11970560 | tf_op jit(solution)/shard_map/tf,df->td/dot_general | solution.py:162
  297.6 37.4 %reduce-scatter.2.cloned.1.call-done = bf16[96,1792]{1,0:T(8,128)(2,1)} async-done(((bf16[768,1792]{1,0:T(8,128)(2,1)}), bf16[96,1792]{1,0:T(8,128)(2,1)}) %reduce-scatter.2.cloned.1.call-update) | async-done | bytes 344080 | tf_op jit(solution)/shard_map/reduce_scatter | solution.py:166
  335.0 1.9 add_convert_fusion.1
  (86 shorter events, 11.0 us)
Async XLA Ops:
  6.5 59.6 %copy-start = (bf16[3,224,1792]{2,1,0:T(8,128)(2,1)S(1)}, bf16[3,224,1792]{2,1,0:T(8,128)(2,1)}, u32[]{:S(2)}) copy-start(bf16[3,224,1792]{2,1,0:T(8,128)(2,1)} %param.16) | copy-start | bytes 7225348
  6.5 167.8 %all-gather.3.cloned.1.call-start = ((), (), s32[]{:S(2)}) async-start(), calls=%async_computation.2 | async-start | bytes 7096320 | tf_op jit(solution)/shard_map/all_gather | solution.py:108
  36.2 13.0 %copy-start.11 = (s32[1,24]{1,0:T(1,128)S(1)}, s32[1,24]{1,0:T(1,128)}, u32[]{:S(2)}) copy-start(s32[1,24]{1,0:T(1,128)} %param.25) | copy-start | bytes 292
  36.2 13.4 %copy-start.9 = (s32[768]{0:T(1024)S(1)}, s32[768]{0:T(1024)}, u32[]{:S(2)}) copy-start(s32[768]{0:T(1024)} %param.24) | copy-start | bytes 9220
  36.3 13.5 %copy-start.6 = (bf16[8,1792,16]{1,2,0:T(8,128)(2,1)S(1)}, bf16[8,1792,16]{1,2,0:T(8,128)(2,1)}, u32[]{:S(2)}) copy-start(bf16[8,1792,16]{1,2,0:T(8,128)(2,1)} %param.18) | copy-start | bytes 1376260
  36.3 138.1 %all-to-all-start = ((bf16[32,2,2,224,64]{3,2,4,1,0:T(2,128)(2,1)}), bf16[32,2,2,224,64]{3,2,4,1,0:T(2,128)(2,1)}, u32[]{:S(2)}, u32[]{:S(2)}) async-start(bf16[32,2,2,224,64]{3,2,4,1,0:T(2,128)(2,1)} %bitcast.77), calls=%async_computation | async-start | bytes 8388608 | tf_op jit(solution)/shard_map/all_to_all | solution.py:107
  49.2 227.5 %all-reduce.2.cloned.1.call-start = ((), (), s32[]{:S(2)}) async-start(), calls=%async_computation.3 | async-start | bytes 5505024 | tf_op jit(solution)/shard_map/psum | solution.py:152
  49.7 16.4 %copy-start.2 = (bf16[768,1792]{1,0:T(8,128)(2,1)S(1)}, bf16[768,1792]{1,0:T(8,128)(2,1)}, u32[]{:S(2)}) copy-start(bf16[768,1792]{1,0:T(8,128)(2,1)} %param.15) | copy-start | bytes 8257540
  66.1 5.2 %copy-start.12 = (f32[4]{0:T(128)S(1)}, f32[4]{0:T(128)}, u32[]{:S(2)}) copy-start(f32[4]{0:T(128)} %param.20) | copy-start | bytes 52
  66.2 5.2 %copy-start.13 = (s32[24]{0:T(128)S(1)}, s32[24]{0:T(128)}, u32[]{:S(2)}) copy-start(s32[24]{0:T(128)} %param.26) | copy-start | bytes 292
  68.2 1.4 copy-start.4
  182.9 1.6 copy-start.8
  184.5 9.6 %copy-start.7 = (bf16[768,2,112]{0,2,1:T(8,128)(2,1)S(1)}, bf16[768,2,112]{0,2,1:T(8,128)(2,1)}, u32[]{:S(2)}) copy-start(bf16[768,2,112]{0,2,1:T(8,128)(2,1)} %get-tuple-element.21) | copy-start | bytes 1032196
  194.1 7.6 %copy-start.5 = (bf16[224,1792]{1,0:T(8,128)(2,1)S(1)}, bf16[224,1792]{1,0:T(8,128)(2,1)}, u32[]{:S(2)}) copy-start(bf16[224,1792]{1,0:T(8,128)(2,1)} %param.17) | copy-start | bytes 2408452
  201.7 2.8 copy-start.10
  204.2 130.8 %reduce-scatter.2.cloned.1.call-start = ((), (), s32[]{:S(2)}) async-start(), calls=%async_computation.4 | async-start | bytes 3096576 | tf_op jit(solution)/shard_map/reduce_scatter | solution.py:166
  280.3 1.6 copy-start.3
  287.0 49.9 %copy-start.1 = (bf16[3,224,1792]{2,1,0:T(8,128)(2,1)S(1)}, bf16[3,224,1792]{2,1,0:T(8,128)(2,1)}, u32[]{:S(2)}) copy-start(bf16[3,224,1792]{2,1,0:T(8,128)(2,1)} %param.16) | copy-start | bytes 7225348
Sparse Core Ops, SparseCore 0:
  10.0 159.9 all-gather.2
  204.3 72.3 all-reduce.1
  297.7 37.2 reduce-scatter.1
